TPU v7x, 512 devices: a whole 4x8x8 slice. The times are simulated.
512 devices in a mesh: stream: 128 (over y, z, core), vert: 4 (over x).
Axes of the slice: x: 4, y: 8, z: 8, core: 2. Of those that a mesh axis runs over, the one named last changes fastest.
Arguments:
- particles: float32 [4096, 4, 7, 128], P('stream', 'vert'), may hold values from -4 to 4, as said below
- phase_flags: int32 [4096, 4, 128], P('stream', 'vert'), may hold values 0 or 1
- neighbours: int32 [4096, 4, 4], P('stream', 'vert'), may hold values from 0 to 7, as said below
- history: bfloat16 [4096, 4, 3, 126, 128], P('stream', 'vert'), may hold values from -160 to 160
- basis_start: float32 [128, 64], replicated, may hold values from -0.5 to 0.5
Outputs:
- new_state: float32 [4096, 4, 7, 128], P('stream', 'vert')
- filtered: float32 [4096, 4, 3, 128], P('stream', 'vert')
Inputs may be any that keep to these rules, and one draw needn't show every extreme that they name: `particles`: rows 0 to 2 of a particle lie in 0 to 2, rows 3 to 5 in -4 to 4, row 6 in 0.97 to 1.03. `neighbours`: the 4 codes of one block are distinct.
All inputs are finite; a program needn't handle non-finite values. No bound on the sum of `phase_flags` on one device may be relied on, other than what follows from the above.
Results may differ from a plain program's by a relative error of at most 0.0003.
Values sent between devices are 32-bit elements; how exact they have to be, the bound alone decides.
A program may use at most 64 MiB of HBM per device.

v0:
```python
import math
import jax
import jax.numpy as jnp
from jax import lax
from jax.sharding import PartitionSpec as P

POD_ITERS = 4
ALPHA_KERNEL = 21.0 / (16.0 * math.pi)
VOLUME = 1.0 / 16.0
STIFFNESS = 100.0 / 7.0
TIME_STEP = 0.02
GRAVITY = 1.0
SEDIMENT_EXTRA = 1.65


def with_halo(block, sides, width):
    for axis, dim in sides:
        count = lax.axis_size(axis)
        forward = [(i, i + 1) for i in range(count - 1)]
        backward = [(target, source) for source, target in forward]
        low = lax.ppermute(
            lax.slice_in_dim(block, block.shape[dim] - width, None, axis=dim), axis, forward
        )
        high = lax.ppermute(lax.slice_in_dim(block, 0, width, axis=dim), axis, backward)
        block = jnp.concatenate([low, block, high], axis=dim)
    return block


def forces(own_block, near_blocks, cell_shifts):
    separation = (
        own_block[:, None, 0:3, :, None]
        - near_blocks[:, :, 0:3, None, :]
        - cell_shifts[:, :, :, None, None]
    )
    radius = jnp.sqrt(jnp.sum(separation * separation, axis=2))
    kernel_reach = jnp.maximum(1.0 - 0.5 * radius, 0.0)
    kernel_slope = -5.0 * ALPHA_KERNEL * kernel_reach**3 * near_blocks[:, :, 6, None, :]
    closing = own_block[:, None, 3:6, :, None] - near_blocks[:, :, 3:6, None, :]
    density_rate = jnp.sum(kernel_slope * jnp.sum(closing * separation, axis=2), axis=(1, 3))
    pressure_term = kernel_slope * (own_block[:, None, 7, :, None] + near_blocks[:, :, 7, None, :])
    acceleration = -jnp.sum(pressure_term[:, :, None] * separation, axis=(1, 4))
    return (acceleration, density_rate)


def block_layout(neighbours):
    blocks_stream, blocks_vert = (neighbours.shape[0], neighbours.shape[1])
    offset_code = neighbours + (neighbours >= 4).astype(jnp.int32)
    zero_codes = jnp.zeros((blocks_stream, blocks_vert, 1), jnp.int32)
    stream_step = jnp.concatenate([zero_codes, offset_code // 3 - 1], axis=-1)
    vert_step = jnp.concatenate([zero_codes, offset_code % 3 - 1], axis=-1)
    stream_place = jnp.arange(blocks_stream, dtype=jnp.int32)[:, None, None]
    vert_place = jnp.arange(blocks_vert, dtype=jnp.int32)[None, :, None]
    near_index = (stream_place + 1 + stream_step) * (blocks_vert + 2) + (vert_place + 1 + vert_step)
    list_width = near_index.shape[2]
    cell_shifts = jnp.stack(
        [
            2.0 * stream_step.astype(jnp.float32),
            jnp.zeros(stream_step.shape, jnp.float32),
            2.0 * vert_step.astype(jnp.float32),
        ],
        axis=-1,
    )
    return (near_index.reshape(-1, list_width), cell_shifts.reshape(-1, list_width, 3))


def make_payload(particles, rest_density, particle_mass):
    relative = particles[:, :, 6]
    pressure = STIFFNESS * (relative**7 - 1.0) / (rest_density * relative * relative)
    return jnp.concatenate(
        [particles[:, :, 0:6], particle_mass[:, :, None], pressure[:, :, None]], axis=2
    )


def interact(payload, extended, near_index, cell_shifts, group_limit):
    block_count = payload.shape[0] * payload.shape[1]
    group_size = math.gcd(block_count, group_limit)
    flat_blocks = extended.reshape(-1, 8, payload.shape[3])
    list_width = near_index.shape[1]

    def one_group(pieces):
        own_block, index_part, shift_part = pieces
        near_blocks = jnp.take(flat_blocks, index_part, axis=0)
        return forces(own_block, near_blocks, shift_part)

    acceleration, density_rate = lax.map(
        one_group,
        (
            payload.reshape(block_count // group_size, group_size, 8, -1),
            near_index.reshape(-1, group_size, list_width),
            cell_shifts.reshape(-1, group_size, list_width, 3),
        ),
    )
    return (
        acceleration.reshape(payload.shape[0], payload.shape[1], 3, -1),
        density_rate.reshape(payload.shape[0], payload.shape[1], -1),
    )


def update(particles, rest_density, acceleration, density_rate):
    gravity_vector = jnp.array([0.0, 0.0, -GRAVITY], jnp.float32)[:, None]
    velocity = particles[:, :, 3:6] + TIME_STEP * (acceleration + gravity_vector)
    position = particles[:, :, 0:3] + TIME_STEP * velocity
    relative = particles[:, :, 6] + TIME_STEP * density_rate / rest_density
    return jnp.concatenate([position, velocity, relative[:, :, None]], axis=2)


def orthonormal(matrix):
    for repeat in range(2):
        inner_product = jnp.dot(matrix.T, matrix, precision=lax.Precision.HIGHEST)
        factor = jnp.linalg.cholesky(inner_product)
        matrix = lax.linalg.triangular_solve(
            factor, matrix, left_side=False, lower=True, transpose_a=True
        )
    return matrix


def pod_weights(gram_matrix, basis_start):
    basis_now = orthonormal(basis_start)
    for iteration in range(POD_ITERS):
        basis_now = orthonormal(jnp.dot(gram_matrix, basis_now, precision=lax.Precision.HIGHEST))
    return jnp.dot(basis_now, basis_now[-1], precision=lax.Precision.HIGHEST)


def extend(payload):
    return with_halo(payload, (("stream", 0), ("vert", 1)), 1)


def advance(particles, rest_density, particle_mass, near_index, cell_shifts):
    payload = make_payload(particles, rest_density, particle_mass)
    extended = extend(payload)
    acceleration, density_rate = interact(payload, extended, near_index, cell_shifts, 4)
    return update(particles, rest_density, acceleration, density_rate)


def body(particles, phase_flags, neighbours, history, basis_start):
    rest_density = 1.0 + SEDIMENT_EXTRA * phase_flags.astype(jnp.float32)
    particle_mass = rest_density * VOLUME
    near_index, cell_shifts = block_layout(neighbours)
    first_state = advance(particles, rest_density, particle_mass, near_index, cell_shifts)
    second_state = advance(first_state, rest_density, particle_mass, near_index, cell_shifts)
    new_snapshots = jnp.stack([first_state[:, :, 3:6], second_state[:, :, 3:6]], axis=3).astype(
        jnp.bfloat16
    )
    snapshots = jnp.concatenate([history, new_snapshots], axis=3)
    gram_matrix = lax.psum(
        jnp.einsum("abcsp,abctp->st", snapshots, snapshots, preferred_element_type=jnp.float32),
        ("stream", "vert"),
    )
    weights = pod_weights(gram_matrix, basis_start)
    filtered = jnp.einsum(
        "abcsp,s->abcp", snapshots.astype(jnp.float32), weights, precision=lax.Precision.HIGHEST
    )
    return (second_state, filtered)


def solution(mesh):
    in_specs = (
        P("stream", "vert", None, None),
        P("stream", "vert", None),
        P("stream", "vert", None),
        P("stream", "vert", None, None, None),
        P(),
    )
    out_specs = (P("stream", "vert", None, None), P("stream", "vert", None, None))
    return jax.shard_map(body, mesh=mesh, in_specs=in_specs, out_specs=out_specs, check_vma=False)
```

profile of v0, /device:TPU:1, one launch (start us, length us, event | category | flops | bytes accessed | tf_op | source)
XLA Modules:
  0.0 584.5 jit_solution(12489457789824271340)
XLA Ops:
  9.6 5.4 collective-permute-start
  21.8 5.8 %cholesky.164 = f32[64,64]{1,0:T(8,128)S(1)} custom-call(f32[64,64]{1,0:T(8,128)S(1)} %fusion.36), custom_call_target="Cholesky" | custom-call | tf_op jit(solution)/shard_map/jit(cholesky)/cholesky | solution.py:110
  29.0 4.9 custom-call.14
  34.4 5.8 %cholesky.175 = f32[64,64]{1,0:T(8,128)S(1)} custom-call(f32[64,64]{1,0:T(8,128)S(1)} %fusion.34), custom_call_target="Cholesky" | custom-call | tf_op jit(solution)/shard_map/jit(cholesky)/cholesky | solution.py:110
  50.5 48.7 %while.24 = (s32[]{:T(128)}, f32[8,4,3,128]{3,2,1,0:T(4,128)S(1)}, f32[8,4,128]{2,1,0:T(4,128)S(1)}, f32[8,4,8,128]{3,1,0,2:T(4,128)S(1)}, s32[8,4,5]{2,1,0:T(4,...) while((s32[]{:T(128)}, f32[8,4,3,128]{3,2,1,0:T(4,128)S(1)}, ...), condition=%wide.region_5.7_spmd, body=%wide.region_0.6_spmd.sunk | while | flops 15424634 | bytes 10094649 | solution.py:85
  106.3 4.9 custom-call.15
  123.3 74.8 %while.25 = (s32[]{:T(128)}, f32[8,4,3,128]{3,2,1,0:T(4,128)}, f32[8,4,128]{2,1,0:T(4,128)}, f32[8,4,8,128]{3,1,2,0:T(4,128)}, s32[8,4,5]{2,1,0:T(4,128)}, /*ind...) while((s32[]{:T(128)}, f32[8,4,3,128]{3,2,1,0:T(4,128)}, f32[8,4,128]{2,1,0:T(4,128)}, ...), condition=%wide.region_11.13_spmd, body=%wide.region_6.12_spmd.sunk | while | flops 15424634 | bytes 10093617 | solution.py:85
  202.5 268.8 %all-reduce.4.cloned.1.call-done = f32[128,128]{1,0:T(8,128)} async-done(((f32[128,128]{1,0:T(8,128)}), f32[128,128]{1,0:T(8,128)}) %all-reduce.4.cloned.1.call-update) | async-done | bytes 65552 | tf_op jit(solution)/shard_map/psum | solution.py:145
  472.7 5.8 %cholesky.186 = f32[64,64]{1,0:T(8,128)S(1)} custom-call(f32[64,64]{1,0:T(8,128)S(1)} %fusion.32), custom_call_target="Cholesky" | custom-call | tf_op jit(solution)/shard_map/jit(cholesky)/cholesky | solution.py:110
  479.9 4.9 custom-call.16
  485.4 5.8 %cholesky.197 = f32[64,64]{1,0:T(8,128)S(1)} custom-call(f32[64,64]{1,0:T(8,128)S(1)} %fusion.30), custom_call_target="Cholesky" | custom-call | tf_op jit(solution)/shard_map/jit(cholesky)/cholesky | solution.py:110
  492.6 4.9 custom-call.17
  499.1 5.8 %cholesky.208 = f32[64,64]{1,0:T(8,128)S(1)} custom-call(f32[64,64]{1,0:T(8,128)S(1)} %fusion.28), custom_call_target="Cholesky" | custom-call | tf_op jit(solution)/shard_map/jit(cholesky)/cholesky | solution.py:110
  506.3 4.9 custom-call.18
  511.7 5.8 %cholesky.219 = f32[64,64]{1,0:T(8,128)S(1)} custom-call(f32[64,64]{1,0:T(8,128)S(1)} %fusion.26), custom_call_target="Cholesky" | custom-call | tf_op jit(solution)/shard_map/jit(cholesky)/cholesky | solution.py:110
  518.9 4.9 custom-call.19
  524.6 5.8 %cholesky.230 = f32[64,64]{1,0:T(8,128)S(1)} custom-call(f32[64,64]{1,0:T(8,128)S(1)} %fusion.24), custom_call_target="Cholesky" | custom-call | tf_op jit(solution)/shard_map/jit(cholesky)/cholesky | solution.py:110
  531.8 4.9 custom-call.20
  537.2 6.0 %cholesky.241 = f32[64,64]{1,0:T(8,128)S(1)} custom-call(f32[64,64]{1,0:T(8,128)S(1)} %fusion.22), custom_call_target="Cholesky" | custom-call | tf_op jit(solution)/shard_map/jit(cholesky)/cholesky | solution.py:110
  544.6 4.9 custom-call.21
  550.3 5.8 %cholesky.252 = f32[64,64]{1,0:T(8,128)S(1)} custom-call(f32[64,64]{1,0:T(8,128)S(1)} %fusion.20), custom_call_target="Cholesky" | custom-call | tf_op jit(solution)/shard_map/jit(cholesky)/cholesky | solution.py:110
  557.4 4.9 custom-call.22
  562.9 5.8 %cholesky.263 = f32[64,64]{1,0:T(8,128)S(1)} custom-call(f32[64,64]{1,0:T(8,128)S(1)} %fusion.18), custom_call_target="Cholesky" | custom-call | tf_op jit(solution)/shard_map/jit(cholesky)/cholesky | solution.py:110
  570.1 4.9 custom-call.23
  (561 shorter events, 185.8 us)
Async XLA Ops:
  7.2 14.3 %copy-start = (f32[128,64]{0,1:T(8,128)S(1)}, f32[128,64]{0,1:T(8,128)}, u32[]{:S(2)}) copy-start(f32[128,64]{0,1:T(8,128)} %param.20) | copy-start | bytes 98308
  7.2 464.1 %all-reduce.4.cloned.1.call-start = ((), (), s32[]{:S(2)}) async-start(), calls=%async_computation | async-start | bytes 131072 | tf_op jit(solution)/shard_map/psum | solution.py:145
  9.6 30.8 %collective-permute-start = (f32[1,1,8,128]{3,0,2,1:T(1,128)S(1)}, f32[1,1,8,128]{3,0,2,1:T(1,128)S(1)}, u32[]{:S(2)}, u32[]{:S(2)}) collective-permute-start(f32[1,1,8,128]{3,0,2,1:T(1,128)S(1)} %get-tuple-element.168), channel_id=1, source_target_pairs={{0,4},{4,8},{8,12},{12,16},{16,20},{20,24},{24,28},{28,32},{32,36}... | collective-permute-start | bytes 12296 | tf_op jit(solution)/shard_map/ppermute | solution.py:21
  15.0 25.4 %collective-permute-start.1 = (f32[1,1,8,128]{3,0,2,1:T(1,128)S(1)}, f32[1,1,8,128]{3,0,2,1:T(1,128)S(1)}, u32[]{:S(2)}, u32[]{:S(2)}) collective-permute-start(f32[1,1,8,128]{3,0,2,1:T(1,128)S(1)} %get-tuple-element.169), channel_id=1, source_target_pairs={{4,0},{8,4},{12,8},{16,12},{20,16},{24,20},{28,24},{32,28},{36,32}... | collective-permute-start | bytes 12296 | tf_op jit(solution)/shard_map/ppermute | solution.py:24
  40.5 4.9 collective-permute-start.2
  41.8 7.8 %collective-permute-start.3 = (f32[34,1,8,128]{3,0,2,1:T(8,128)S(1)}, f32[34,1,8,128]{3,0,2,1:T(8,128)S(1)}, u32[]{:S(2)}, u32[]{:S(2)}) collective-permute-start(f32[34,1,8,128]{3,0,2,1:T(8,128)S(1)} %pad_maximum_fusion.2), channel_id=1, source_target_pairs={{1,0},{2,1},{3,2},{5,4},{6,5},{7,6},{9,8},{10,9},{11,10},{13,12},{... | collective-permute-start | bytes 417800 | tf_op jit(solution)/shard_map/ppermute | solution.py:24
  50.5 48.8 %copy-start.3 = (s32[32,1,128]{2,1,0:T(1,128)S(1)}, s32[32,1,128]{2,1,0:T(1,128)}, u32[]{:S(2)}) copy-start(s32[32,1,128]{2,1,0:T(1,128)} %param.17) | copy-start | bytes 49156
  50.5 49.4 %copy-start.10 = (f32[3]{0:T(128)S(1)}, f32[3]{0:T(128)}, u32[]{:S(2)}) copy-start(f32[3]{0:T(128)} %constant.134.clone) | copy-start | bytes 40
  99.2 0.6 copy-start.2
  99.2 16.7 %copy-start.7 = (s32[8,4,5]{2,1,0:T(4,128)}, s32[8,4,5]{2,1,0:T(4,128)S(1)}, u32[]{:S(2)}) copy-start(s32[8,4,5]{2,1,0:T(4,128)S(1)} %get-tuple-element.364) | copy-start | bytes 1924
  99.2 0.6 copy-start.4
  100.0 11.2 %collective-permute-start.4 = (f32[1,1,8,128]{3,2,1,0:T(8,128)S(1)}, f32[1,1,8,128]{3,2,1,0:T(8,128)S(1)}, u32[]{:S(2)}, u32[]{:S(2)}) collective-permute-start(f32[1,1,8,128]{3,2,1,0:T(8,128)S(1)} %get-tuple-element.166), channel_id=1, source_target_pairs={{0,4},{4,8},{8,12},{12,16},{16,20},{20,24},{24,28},{28,32},{32,36}... | collective-permute-start | bytes 12296 | tf_op jit(solution)/shard_map/ppermute | solution.py:21
  103.7 7.5 %collective-permute-start.5 = (f32[1,1,8,128]{3,2,1,0:T(8,128)S(1)}, f32[1,1,8,128]{3,2,1,0:T(8,128)S(1)}, u32[]{:S(2)}, u32[]{:S(2)}) collective-permute-start(f32[1,1,8,128]{3,2,1,0:T(8,128)S(1)} %get-tuple-element.167), channel_id=1, source_target_pairs={{4,0},{8,4},{12,8},{16,12},{20,16},{24,20},{28,24},{32,28},{36,32}... | collective-permute-start | bytes 12296 | tf_op jit(solution)/shard_map/ppermute | solution.py:24
  111.3 9.9 %collective-permute-start.6 = (f32[34,1,8,128]{3,2,1,0:T(8,128)S(1)}, f32[34,1,8,128]{3,2,1,0:T(8,128)S(1)}, u32[]{:S(2)}, u32[]{:S(2)}) collective-permute-start(f32[34,1,8,128]{3,2,1,0:T(8,128)S(1)} %pad_maximum_fusion.3), channel_id=1, source_target_pairs={{0,1},{1,2},{2,3},{4,5},{5,6},{6,7},{8,9},{9,10},{10,11},{12,13},{... | collective-permute-start | bytes 417800 | tf_op jit(solution)/shard_map/ppermute | solution.py:21
  114.4 6.8 %collective-permute-start.7 = (f32[34,1,8,128]{3,2,1,0:T(8,128)S(1)}, f32[34,1,8,128]{3,2,1,0:T(8,128)S(1)}, u32[]{:S(2)}, u32[]{:S(2)}) collective-permute-start(f32[34,1,8,128]{3,2,1,0:T(8,128)S(1)} %pad_maximum_fusion.3), channel_id=1, source_target_pairs={{1,0},{2,1},{3,2},{5,4},{6,5},{7,6},{9,8},{10,9},{11,10},{13,12},{... | collective-permute-start | bytes 417800 | tf_op jit(solution)/shard_map/ppermute | solution.py:24
  199.0 2.6 copy-start.8
  199.0 2.6 copy-start.5
  199.1 272.2 %copy-start.6 = (f32[128,64]{0,1:T(8,128)S(1)}, f32[128,64]{0,1:T(8,128)}, u32[]{:S(2)}) copy-start(f32[128,64]{0,1:T(8,128)} %convolution_bitcast_fusion.8) | copy-start | bytes 98308
  471.3 52.8 %copy-start.1 = (f32[128,128]{1,0:T(8,128)S(1)}, f32[128,128]{1,0:T(8,128)}, u32[]{:S(2)}) copy-start(f32[128,128]{1,0:T(8,128)} %all-reduce.4.cloned.1.call-done) | copy-start | bytes 196612
  511.4 64.1 %copy-start.9 = (bf16[32,1,3,1,128]{4,3,2,0,1:T(2,128)(2,1)S(1)}, bf16[32,1,3,1,128]{4,3,2,0,1:T(2,128)(2,1)}, u32[]{:S(2)}) copy-start(bf16[32,1,3,1,128]{4,3,2,0,1:T(2,128)(2,1)} %copy.167) | copy-start | bytes 73732
Sparse Core Ops, SparseCore 0:
  201.7 269.5 all-reduce.3
where the time goes:
time: 587 us; the launch traced here: 584 us
  waiting for transfers between devices  275 us (47%)
  other arithmetic  200 us (34%)
  local copies, waits for them, and re-layouts  58.8 us (10%)
  starting transfers between devices  22.9 us (4%)
  between operations  14.9 us (3%)
  matrix products  11.6 us (2%)
    psum x1, waiting for transfers between devices, body(): lax.psum(jnp.einsum('abcsp,abctp->st', snapshots, snapshots, preferred_el...  269 us
    another operation x30, other arithmetic, orthonormal(): factor = jnp.linalg.cholesky(inner_product)  65.3 us
    another operation x20, other arithmetic, orthonormal(): lax.linalg.triangular_solve(factor, matrix, left_side=False, lower=True,...  55.5 us
    reduce_sum x16, other arithmetic, forces(): jnp.sum(closing * separation, axis=2)  28.4 us
    gather x16, local copies, waits for them, and re-layouts, one_group(): near_blocks = jnp.take(flat_blocks, index_part, axis=0)  25 us
    ppermute x4, starting transfers between devices, with_halo(): lax.ppermute(lax.slice_in_dim(block, block.shape[dim] - width, None, axis...  13.5 us
    reduce_sum x16, other arithmetic, forces(): radius = jnp.sqrt(jnp.sum(separation * separation, axis=2))  11.9 us
  transfers between devices with their start and end apart: 9, of which 3 were waited for; matrix products, arithmetic and copies ran while one was open for 6% of the time, Pallas kernels for 0%

commit v1 on v0

--- a/solution.py
+++ b/solution.py
@@ -1,3 +1,4 @@
+import functools
 import math
 import jax
 import jax.numpy as jnp
@@ -11,6 +12,15 @@
 TIME_STEP = 0.02
 GRAVITY = 1.0
 SEDIMENT_EXTRA = 1.65
+
+
+def tasks_pass(sheet, bus_axis, dev_axis):
+    for k0 in (bus_axis, dev_axis):
+        sheet = jax.lax.psum(sheet, k0)
+    return sheet
+
+
+_feed_rounds = functools.partial(tasks_pass, bus_axis="vert", dev_axis="stream")
 
 
 def with_halo(block, sides, width):
@@ -142,9 +152,8 @@
         jnp.bfloat16
     )
     snapshots = jnp.concatenate([history, new_snapshots], axis=3)
-    gram_matrix = lax.psum(
-        jnp.einsum("abcsp,abctp->st", snapshots, snapshots, preferred_element_type=jnp.float32),
-        ("stream", "vert"),
+    gram_matrix = _feed_rounds(
+        jnp.einsum("abcsp,abctp->st", snapshots, snapshots, preferred_element_type=jnp.float32)
     )
     weights = pod_weights(gram_matrix, basis_start)
     filtered = jnp.einsum(

time: 587 us -> 561 us (0.956)
  waiting for transfers between devices: 275 us -> 249 us
  local copies, waits for them, and re-layouts: 58.8 us -> 50.2 us
  other arithmetic: 200 us -> 207 us
    psum x1 -> x2, waiting for transfers between devices: 269 us -> 244 us  [tasks_pass(): sheet = jax.lax.psum(sheet, k0)]
    gather x16, local copies, waits for them, and re-layouts: 25 us -> 17.1 us  [one_group(): near_blocks = jnp.take(flat_blocks, index_part, axis=0)]
  transfers between devices with their start and end apart: 9 -> 10, of which waited for: 3 -> 4; matrix products, arithmetic and copies ran while one was open for 6% -> 6% of each run, Pallas kernels for 0% -> 0%
where the time goes in v1:
time: 561 us; the launch traced here: 558 us
  waiting for transfers between devices  249 us (44%)
  other arithmetic  207 us (37%)
  local copies, waits for them, and re-layouts  50.2 us (9%)
  starting transfers between devices  23.1 us (4%)
  between operations  14.9 us (3%)
  matrix products  11.6 us (2%)
    psum x2, waiting for transfers between devices, tasks_pass(): sheet = jax.lax.psum(sheet, k0)  244 us
    another operation x30, other arithmetic, orthonormal(): factor = jnp.linalg.cholesky(inner_product)  65.6 us
    another operation x20, other arithmetic, orthonormal(): lax.linalg.triangular_solve(factor, matrix, left_side=False, lower=True,...  55.7 us
    reduce_sum x16, other arithmetic, forces(): jnp.sum(closing * separation, axis=2)  29.2 us
    gather x16, local copies, waits for them, and re-layouts, one_group(): near_blocks = jnp.take(flat_blocks, index_part, axis=0)  17.1 us
    ppermute x4, starting transfers between devices, with_halo(): lax.ppermute(lax.slice_in_dim(block, block.shape[dim] - width, None, axis...  13.5 us
    reduce_sum x16, other arithmetic, forces(): radius = jnp.sqrt(jnp.sum(separation * separation, axis=2))  12.1 us
    reduce_sum x16, other arithmetic, forces(): jnp.sum(kernel_slope * jnp.sum(closing * separation, axis=2), axis=(1, 3))  11.6 us
  transfers between devices with their start and end apart: 10, of which 4 were waited for; matrix products, arithmetic and copies ran while one was open for 6% of the time, Pallas kernels for 0%

profile of v1, /device:TPU:1, one launch (start us, length us, event | category | flops | bytes accessed | tf_op | source)
XLA Modules:
  0.0 558.4 jit_solution(14935533596909725406)
XLA Ops:
  9.6 5.4 collective-permute-start
  21.8 5.8 %cholesky.164 = f32[64,64]{1,0:T(8,128)S(1)} custom-call(f32[64,64]{1,0:T(8,128)S(1)} %fusion.36), custom_call_target="Cholesky" | custom-call | tf_op jit(solution)/shard_map/jit(cholesky)/cholesky | solution.py:120
  29.0 4.9 custom-call.14
  34.4 5.8 %cholesky.175 = f32[64,64]{1,0:T(8,128)S(1)} custom-call(f32[64,64]{1,0:T(8,128)S(1)} %fusion.34), custom_call_target="Cholesky" | custom-call | tf_op jit(solution)/shard_map/jit(cholesky)/cholesky | solution.py:120
  49.8 47.1 %while.24 = (s32[]{:T(128)}, f32[8,4,3,128]{3,2,1,0:T(4,128)S(1)}, f32[8,4,128]{2,1,0:T(4,128)S(1)}, f32[8,4,8,128]{3,1,0,2:T(4,128)S(1)}, s32[8,4,5]{2,1,0:T(4,...) while((s32[]{:T(128)}, f32[8,4,3,128]{3,2,1,0:T(4,128)S(1)}, ...), condition=%wide.region_5.7_spmd, body=%wide.region_0.6_spmd.sunk | while | flops 15424634 | bytes 10094649 | solution.py:95
  104.0 4.9 custom-call.15
  121.0 75.0 %while.25 = (s32[]{:T(128)}, f32[8,4,3,128]{3,2,1,0:T(4,128)}, f32[8,4,128]{2,1,0:T(4,128)}, f32[8,4,8,128]{3,1,2,0:T(4,128)}, s32[8,4,5]{2,1,0:T(4,128)}, /*ind...) while((s32[]{:T(128)}, f32[8,4,3,128]{3,2,1,0:T(4,128)}, f32[8,4,128]{2,1,0:T(4,128)}, ...), condition=%wide.region_11.13_spmd, body=%wide.region_6.12_spmd.sunk | while | flops 15424634 | bytes 10109033 | solution.py:95
  199.9 55.7 %all-reduce.5.cloned.1.call-done = f32[128,128]{1,0:T(8,128)} async-done(((f32[128,128]{1,0:T(8,128)}), f32[128,128]{1,0:T(8,128)}) %all-reduce.5.cloned.1.call-update) | async-done | bytes 65552 | tf_op jit(solution)/shard_map/psum | solution.py:19
  256.4 188.5 %all-reduce.7.cloned.1.call-done = f32[128,128]{1,0:T(8,128)} async-done(((f32[128,128]{1,0:T(8,128)}), f32[128,128]{1,0:T(8,128)}) %all-reduce.7.cloned.1.call-update) | async-done | bytes 65552 | tf_op jit(solution)/shard_map/psum | solution.py:19
  446.3 5.8 %cholesky.186 = f32[64,64]{1,0:T(8,128)S(1)} custom-call(f32[64,64]{1,0:T(8,128)S(1)} %fusion.32), custom_call_target="Cholesky" | custom-call | tf_op jit(solution)/shard_map/jit(cholesky)/cholesky | solution.py:120
  453.5 4.9 custom-call.16
  458.9 5.8 %cholesky.197 = f32[64,64]{1,0:T(8,128)S(1)} custom-call(f32[64,64]{1,0:T(8,128)S(1)} %fusion.30), custom_call_target="Cholesky" | custom-call | tf_op jit(solution)/shard_map/jit(cholesky)/cholesky | solution.py:120
  466.1 4.9 custom-call.17
  472.6 5.8 %cholesky.208 = f32[64,64]{1,0:T(8,128)S(1)} custom-call(f32[64,64]{1,0:T(8,128)S(1)} %fusion.28), custom_call_target="Cholesky" | custom-call | tf_op jit(solution)/shard_map/jit(cholesky)/cholesky | solution.py:120
  479.8 4.9 custom-call.18
  485.2 5.8 %cholesky.219 = f32[64,64]{1,0:T(8,128)S(1)} custom-call(f32[64,64]{1,0:T(8,128)S(1)} %fusion.26), custom_call_target="Cholesky" | custom-call | tf_op jit(solution)/shard_map/jit(cholesky)/cholesky | solution.py:120
  492.4 4.9 custom-call.19
  498.1 5.8 %cholesky.230 = f32[64,64]{1,0:T(8,128)S(1)} custom-call(f32[64,64]{1,0:T(8,128)S(1)} %fusion.24), custom_call_target="Cholesky" | custom-call | tf_op jit(solution)/shard_map/jit(cholesky)/cholesky | solution.py:120
  510.9 5.8 %cholesky.241 = f32[64,64]{1,0:T(8,128)S(1)} custom-call(f32[64,64]{1,0:T(8,128)S(1)} %fusion.22), custom_call_target="Cholesky" | custom-call | tf_op jit(solution)/shard_map/jit(cholesky)/cholesky | solution.py:120
  518.2 5.0 custom-call.21
  524.0 5.8 %cholesky.252 = f32[64,64]{1,0:T(8,128)S(1)} custom-call(f32[64,64]{1,0:T(8,128)S(1)} %fusion.20), custom_call_target="Cholesky" | custom-call | tf_op jit(solution)/shard_map/jit(cholesky)/cholesky | solution.py:120
  531.3 4.9 custom-call.22
  536.8 5.8 %cholesky.263 = f32[64,64]{1,0:T(8,128)S(1)} custom-call(f32[64,64]{1,0:T(8,128)S(1)} %fusion.18), custom_call_target="Cholesky" | custom-call | tf_op jit(solution)/shard_map/jit(cholesky)/cholesky | solution.py:120
  544.1 4.9 custom-call.23
  (598 shorter events, 189.3 us)
Async XLA Ops:
  7.2 14.3 %copy-start = (f32[128,64]{0,1:T(8,128)S(1)}, f32[128,64]{0,1:T(8,128)}, u32[]{:S(2)}) copy-start(f32[128,64]{0,1:T(8,128)} %param.20) | copy-start | bytes 98308
  7.2 248.4 %all-reduce.5.cloned.1.call-start = ((), (), s32[]{:S(2)}) async-start(), calls=%async_computation | async-start | bytes 131072 | tf_op jit(solution)/shard_map/psum | solution.py:19
  9.6 30.8 %collective-permute-start = (f32[1,1,8,128]{3,0,2,1:T(1,128)S(1)}, f32[1,1,8,128]{3,0,2,1:T(1,128)S(1)}, u32[]{:S(2)}, u32[]{:S(2)}) collective-permute-start(f32[1,1,8,128]{3,0,2,1:T(1,128)S(1)} %get-tuple-element.168), channel_id=1, source_target_pairs={{0,4},{4,8},{8,12},{12,16},{16,20},{20,24},{24,28},{28,32},{32,36}... | collective-permute-start | bytes 12296 | tf_op jit(solution)/shard_map/ppermute | solution.py:31
  15.0 25.4 %collective-permute-start.1 = (f32[1,1,8,128]{3,0,2,1:T(1,128)S(1)}, f32[1,1,8,128]{3,0,2,1:T(1,128)S(1)}, u32[]{:S(2)}, u32[]{:S(2)}) collective-permute-start(f32[1,1,8,128]{3,0,2,1:T(1,128)S(1)} %get-tuple-element.169), channel_id=1, source_target_pairs={{4,0},{8,4},{12,8},{16,12},{20,16},{24,20},{28,24},{32,28},{36,32}... | collective-permute-start | bytes 12296 | tf_op jit(solution)/shard_map/ppermute | solution.py:34
  40.5 4.9 collective-permute-start.2
  41.8 7.8 %collective-permute-start.3 = (f32[34,1,8,128]{3,0,2,1:T(8,128)S(1)}, f32[34,1,8,128]{3,0,2,1:T(8,128)S(1)}, u32[]{:S(2)}, u32[]{:S(2)}) collective-permute-start(f32[34,1,8,128]{3,0,2,1:T(8,128)S(1)} %pad_maximum_fusion.2), channel_id=1, source_target_pairs={{1,0},{2,1},{3,2},{5,4},{6,5},{7,6},{9,8},{10,9},{11,10},{13,12},{... | collective-permute-start | bytes 417800 | tf_op jit(solution)/shard_map/ppermute | solution.py:34
  49.8 47.1 %copy-start.4 = (s32[32,1,128]{2,1,0:T(1,128)S(1)}, s32[32,1,128]{2,1,0:T(1,128)}, u32[]{:S(2)}) copy-start(s32[32,1,128]{2,1,0:T(1,128)} %param.17) | copy-start | bytes 49156
  49.8 47.2 %copy-start.13 = (f32[3]{0:T(128)S(1)}, f32[3]{0:T(128)}, u32[]{:S(2)}) copy-start(f32[3]{0:T(128)} %constant.134.clone) | copy-start | bytes 40
  96.9 20.7 %copy-start.5 = (f32[8,4,128]{2,1,0:T(4,128)}, f32[8,4,128]{2,1,0:T(4,128)S(1)}, u32[]{:S(2)}) copy-start(f32[8,4,128]{2,1,0:T(4,128)S(1)} %broadcast_multiply_fusion.1) | copy-start | bytes 49156
  97.7 11.2 %collective-permute-start.4 = (f32[1,1,8,128]{3,2,1,0:T(8,128)S(1)}, f32[1,1,8,128]{3,2,1,0:T(8,128)S(1)}, u32[]{:S(2)}, u32[]{:S(2)}) collective-permute-start(f32[1,1,8,128]{3,2,1,0:T(8,128)S(1)} %get-tuple-element.166), channel_id=1, source_target_pairs={{0,4},{4,8},{8,12},{12,16},{16,20},{20,24},{24,28},{28,32},{32,36}... | collective-permute-start | bytes 12296 | tf_op jit(solution)/shard_map/ppermute | solution.py:31
  101.4 7.5 %collective-permute-start.5 = (f32[1,1,8,128]{3,2,1,0:T(8,128)S(1)}, f32[1,1,8,128]{3,2,1,0:T(8,128)S(1)}, u32[]{:S(2)}, u32[]{:S(2)}) collective-permute-start(f32[1,1,8,128]{3,2,1,0:T(8,128)S(1)} %get-tuple-element.167), channel_id=1, source_target_pairs={{4,0},{8,4},{12,8},{16,12},{20,16},{24,20},{28,24},{32,28},{36,32}... | collective-permute-start | bytes 12296 | tf_op jit(solution)/shard_map/ppermute | solution.py:34
  109.0 9.9 %collective-permute-start.6 = (f32[34,1,8,128]{3,2,1,0:T(8,128)S(1)}, f32[34,1,8,128]{3,2,1,0:T(8,128)S(1)}, u32[]{:S(2)}, u32[]{:S(2)}) collective-permute-start(f32[34,1,8,128]{3,2,1,0:T(8,128)S(1)} %pad_maximum_fusion.3), channel_id=1, source_target_pairs={{0,1},{1,2},{2,3},{4,5},{5,6},{6,7},{8,9},{9,10},{10,11},{12,13},{... | collective-permute-start | bytes 417800 | tf_op jit(solution)/shard_map/ppermute | solution.py:31
  112.1 6.8 %collective-permute-start.7 = (f32[34,1,8,128]{3,2,1,0:T(8,128)S(1)}, f32[34,1,8,128]{3,2,1,0:T(8,128)S(1)}, u32[]{:S(2)}, u32[]{:S(2)}) collective-permute-start(f32[34,1,8,128]{3,2,1,0:T(8,128)S(1)} %pad_maximum_fusion.3), channel_id=1, source_target_pairs={{1,0},{2,1},{3,2},{5,4},{6,5},{7,6},{9,8},{10,9},{11,10},{13,12},{... | collective-permute-start | bytes 417800 | tf_op jit(solution)/shard_map/ppermute | solution.py:34
  114.4 3.1 copy-start.8
  158.4 2.4 copy-start.2
  177.2 2.4 copy-start.2
  197.0 2.5 copy-start.11
  197.0 2.8 copy-start.9
  197.0 2.9 copy-start.6
  197.0 247.9 %copy-start.7 = (f32[128,64]{0,1:T(8,128)S(1)}, f32[128,64]{0,1:T(8,128)}, u32[]{:S(2)}) copy-start(f32[128,64]{0,1:T(8,128)} %convolution_bitcast_fusion.8) | copy-start | bytes 98308
  199.5 245.3 %all-reduce.7.cloned.1.call-start = ((), (), s32[]{:S(2)}) async-start(), calls=%async_computation.1 | async-start | bytes 131072 | tf_op jit(solution)/shard_map/psum | solution.py:19
  444.8 52.7 %copy-start.1 = (f32[128,128]{1,0:T(8,128)S(1)}, f32[128,128]{1,0:T(8,128)}, u32[]{:S(2)}) copy-start(f32[128,128]{1,0:T(8,128)} %all-reduce.7.cloned.1.call-done) | copy-start | bytes 196612
  484.9 64.6 %copy-start.10 = (bf16[32,1,3,1,128]{4,3,2,0,1:T(2,128)(2,1)S(1)}, bf16[32,1,3,1,128]{4,3,2,0,1:T(2,128)(2,1)}, u32[]{:S(2)}) copy-start(bf16[32,1,3,1,128]{4,3,2,0,1:T(2,128)(2,1)} %copy.167) | copy-start | bytes 73732
  485.0 64.6 %copy-start.12 = (bf16[32,1,3,1,128]{4,3,2,0,1:T(2,128)(2,1)S(1)}, bf16[32,1,3,1,128]{4,3,2,0,1:T(2,128)(2,1)}, u32[]{:S(2)}) copy-start(bf16[32,1,3,1,128]{4,3,2,0,1:T(2,128)(2,1)} %copy-done.11) | copy-start | bytes 73732
  (14 other events, 29.4 us)
Sparse Core Ops, SparseCore 0:
  199.6 55.8 all-reduce.4
  258.8 186.0 all-reduce.6
